TPU v7x, 256 devices: a whole 4x4x8 slice. The times are simulated.
256 devices in a mesh: px: 16 (over y, x), py: 16 (over z, core).
Axes of the slice: x: 4, y: 4, z: 8, core: 2. Of those that a mesh axis runs over, the one named last changes fastest.
Arguments:
- start_field: float32 [128, 256, 512], P('px', 'py'), may hold values from -1.7 to 1.7
- known: float32 [8, 128, 256, 512], P(None, 'px', 'py'), may hold values from -1 to 1
Outputs:
- solution_field: float32 [128, 256, 512], P('px', 'py')
- residual: float32 [128, 256, 512], P('px', 'py')
All inputs are finite; a program needn't handle non-finite values.
Results may differ from a plain program's by a relative error of at most 0.01.
Values sent between devices are 32-bit elements; how exact they have to be, the bound alone decides.
No kernel may reach another device: no remote copies, remote signals or barrier semaphores. Data moves between devices by JAX's collectives and lax.ppermute only.
A program may use at most 64 MiB of HBM per device.

v0:
```python
import jax
import jax.numpy as jnp
from jax import lax
from jax.sharding import PartitionSpec as P

NEWTON = 2
ITERS = 3
DIFFUSION = 0.5
SHIFT = 4.0
EPS = 1e-06


def extended(cells, sides, width):
    for axis, dim in sides:
        count = lax.axis_size(axis)
        ends = count - 1
        head = lax.slice_in_dim(cells, 0, width, axis=dim)
        tail = lax.slice_in_dim(cells, cells.shape[dim] - width, cells.shape[dim], axis=dim)
        cells = jnp.concatenate(
            [
                lax.ppermute(tail, axis, [(i, (i + 1) % count) for i in range(ends)]),
                cells,
                lax.ppermute(head, axis, [((i + 1) % count, i) for i in range(ends)]),
            ],
            axis=dim,
        )
    return cells


def laplace(field):
    padded = extended(field, (("px", 0), ("py", 1)), 1)
    zero = jnp.zeros_like(field[:, :, :1])
    upper = jnp.concatenate([field[:, :, 1:], zero], axis=2)
    lower = jnp.concatenate([zero, field[:, :, :-1]], axis=2)
    beside = padded[2:, 1:-1, :] + padded[:-2, 1:-1, :]
    beside = beside + padded[1:-1, 2:, :] + padded[1:-1, :-2, :]
    return beside + upper + lower - 6.0 * field


def allen_cahn(field, lap):
    return DIFFUSION * lap + field - field * field * field


def solve_small(hess, beta):
    normal = jnp.sum(hess[:, :, None] * hess[:, None, :], axis=0)
    target = beta * hess[0]
    lower = jnp.linalg.cholesky(normal)
    count = normal.shape[0]
    forward = []
    for i in range(count):
        acc = target[i]
        for j in range(i):
            acc = acc - lower[i, j] * forward[j]
        forward.append(acc / lower[i, i])
    back = [None] * count
    for i in reversed(range(count)):
        acc = forward[i]
        for j in range(i + 1, count):
            acc = acc - lower[j, i] * back[j]
        back[i] = acc / lower[i, i]
    return jnp.stack(back)


def local(start_field, known):
    cells = float(
        start_field.shape[0]
        * lax.axis_size("px")
        * start_field.shape[1]
        * lax.axis_size("py")
        * start_field.shape[2]
    )
    field = start_field
    lap_field = laplace(field)
    for step in range(NEWTON):
        force = allen_cahn(field, lap_field)
        diffs = field[None] - known
        dist_local = jnp.sum(diffs * diffs, axis=(1, 2, 3))
        first_sum, force_sq = lax.psum((dist_local, jnp.sum(force * force)), ("px", "py"))
        beta = jnp.sqrt(force_sq + EPS)
        basis = [-force / beta]
        lap_basis = []
        jac_diag = 1.0 - 3.0 * field * field
        hess = jnp.zeros((ITERS + 1, ITERS), jnp.float32)
        for k in range(ITERS):
            lap_vec = laplace(basis[k])
            lap_basis.append(lap_vec)
            image = DIFFUSION * lap_vec + jac_diag * basis[k]
            heights_local = jnp.stack([jnp.sum(vec * image) for vec in basis])
            summed = lax.psum(heights_local, ("px", "py"))
            rest = image
            for j in range(k + 1):
                rest = rest - summed[j] * basis[j]
            height = jnp.sqrt(lax.psum(jnp.sum(rest * rest), ("px", "py")) + EPS)
            hess = hess.at[: k + 1, k].set(summed).at[k + 1, k].set(height)
            if k < ITERS - 1:
                basis.append(rest / height)
        coeffs = solve_small(hess, beta)
        delta = coeffs[0] * basis[0]
        for j in range(1, ITERS):
            delta = delta + coeffs[j] * basis[j]
        inner = lax.psum(jnp.sum(diffs * delta[None], axis=(1, 2, 3)), ("px", "py"))
        mean_dist = first_sum / cells + EPS
        weight = 1.0 / mean_dist + SHIFT
        total = jnp.sum(2.0 * inner / (cells * mean_dist * mean_dist * weight))
        scale = 1.0 / (1.0 + jnp.abs(total))
        field = field + scale * delta
        lap_field = laplace(field)
    return (field, allen_cahn(field, lap_field))


def solution(mesh):
    placed = (P("px", "py", None), P(None, "px", "py", None))
    return jax.shard_map(
        local,
        mesh=mesh,
        in_specs=placed,
        out_specs=(P("px", "py", None), P("px", "py", None)),
        check_vma=False,
    )
```

profile of v0, /device:TPU:38, one launch (start us, length us, event | category | flops | bytes accessed | tf_op | source)
XLA Modules:
  0.0 1435.6 jit_solution(6165251050151356504)
XLA Ops:
  4.2 5.2 collective-permute-start.1
  19.9 80.0 %psum.126 = f32[]{:T(128)} all-reduce(f32[]{:T(128)} %get-tuple-element.179), channel_id=1, replica_groups=mesh['px'=16,'py'=16] {'px','py'}, use_global_device_ids=true, to_apply=%region_1.0 | all-reduce | flops 1 | bytes 8 | tf_op jit(solution)/shard_map/psum | solution.py:78
  107.2 4.7 collective-permute-done.4
  119.8 73.3 %psum.127 = f32[1]{0:T(128)} all-reduce(f32[1]{0:T(128)} %bitcast), channel_id=1, replica_groups=mesh['px'=16,'py'=16] {'px','py'}, use_global_device_ids=true, to_apply=%region_3.0 | all-reduce | flops 1 | bytes 8 | tf_op jit(solution)/shard_map/psum | solution.py:89
  194.5 74.3 %psum.128 = f32[]{:T(128)} all-reduce(f32[]{:T(128)} %multiply_reduce_fusion.21), channel_id=1, replica_groups=mesh['px'=16,'py'=16] {'px','py'}, use_global_device_ids=true, to_apply=%region_5.0 | all-reduce | flops 1 | bytes 8 | tf_op jit(solution)/shard_map/psum | solution.py:93
  291.0 73.4 %psum.129 = f32[2]{0:T(128)S(1)} all-reduce(f32[2]{0:T(128)S(1)} %pad_maximum_fusion.92), channel_id=1, replica_groups=mesh['px'=16,'py'=16] {'px','py'}, use_global_device_ids=true, to_apply=%region_9.0 | all-reduce | flops 2 | bytes 16 | tf_op jit(solution)/shard_map/psum | solution.py:89
  367.1 74.1 %psum.130 = f32[]{:T(128)} all-reduce(f32[]{:T(128)} %get-tuple-element.174), channel_id=1, replica_groups=mesh['px'=16,'py'=16] {'px','py'}, use_global_device_ids=true, to_apply=%region_11.0 | all-reduce | flops 1 | bytes 8 | tf_op jit(solution)/shard_map/psum | solution.py:93
  448.6 4.6 collective-permute-done.12
  466.0 75.2 %psum.131 = f32[3]{0:T(128)S(1)} all-reduce(f32[3]{0:T(128)S(1)} %pad_maximum_fusion.93), channel_id=1, replica_groups=mesh['px'=16,'py'=16] {'px','py'}, use_global_device_ids=true, to_apply=%region_16.0 | all-reduce | flops 3 | bytes 24 | tf_op jit(solution)/shard_map/psum | solution.py:89
  548.8 74.0 %psum.132 = f32[]{:T(128)} all-reduce(f32[]{:T(128)} %multiply_reduce_fusion.14), channel_id=1, replica_groups=mesh['px'=16,'py'=16] {'px','py'}, use_global_device_ids=true, to_apply=%region_18.0 | all-reduce | flops 1 | bytes 8 | tf_op jit(solution)/shard_map/psum | solution.py:93
  636.7 73.7 %all-reduce.21 = (f32[8]{0:T(128)S(1)}, f32[8]{0:T(128)S(1)}) all-reduce(f32[8]{0:T(128)S(1)} %get-tuple-element.150, f32[8]{0:T(128)S(1)} %get-tuple-element.149), channel_id=1, replica_groups=mesh['px'=16,'py'=16] {'px','py'}, use_global_device_ids=true, to_apply=%region_25.27 | all-reduce | flops 16 | bytes 128 | tf_op jit(solution)/shard_map/psum | solution.py:78
  717.7 5.4 collective-permute-done.16
  731.0 73.4 %psum.135 = f32[]{:T(128)} all-reduce(f32[]{:T(128)} %get-tuple-element.171), channel_id=1, replica_groups=mesh['px'=16,'py'=16] {'px','py'}, use_global_device_ids=true, to_apply=%region_28.0 | all-reduce | flops 1 | bytes 8 | tf_op jit(solution)/shard_map/psum | solution.py:78
  811.0 5.4 collective-permute-done.20
  824.3 73.4 %psum.136 = f32[1]{0:T(128)} all-reduce(f32[1]{0:T(128)} %bitcast.32), channel_id=1, replica_groups=mesh['px'=16,'py'=16] {'px','py'}, use_global_device_ids=true, to_apply=%region_30.0 | all-reduce | flops 1 | bytes 8 | tf_op jit(solution)/shard_map/psum | solution.py:89
  899.0 74.1 %psum.137 = f32[]{:T(128)} all-reduce(f32[]{:T(128)} %multiply_reduce_fusion.11), channel_id=1, replica_groups=mesh['px'=16,'py'=16] {'px','py'}, use_global_device_ids=true, to_apply=%region_32.0 | all-reduce | flops 1 | bytes 8 | tf_op jit(solution)/shard_map/psum | solution.py:93
  980.4 5.4 collective-permute-done.24
  995.3 73.4 %psum.138 = f32[2]{0:T(128)S(1)} all-reduce(f32[2]{0:T(128)S(1)} %pad_maximum_fusion.94), channel_id=1, replica_groups=mesh['px'=16,'py'=16] {'px','py'}, use_global_device_ids=true, to_apply=%region_35.0 | all-reduce | flops 2 | bytes 16 | tf_op jit(solution)/shard_map/psum | solution.py:89
  1071.4 74.0 %psum.139 = f32[]{:T(128)} all-reduce(f32[]{:T(128)} %get-tuple-element.166), channel_id=1, replica_groups=mesh['px'=16,'py'=16] {'px','py'}, use_global_device_ids=true, to_apply=%region_37.0 | all-reduce | flops 1 | bytes 8 | tf_op jit(solution)/shard_map/psum | solution.py:93
  1152.9 4.6 collective-permute-done.28
  1170.8 75.2 %psum.140 = f32[3]{0:T(128)S(1)} all-reduce(f32[3]{0:T(128)S(1)} %pad_maximum_fusion.95), channel_id=1, replica_groups=mesh['px'=16,'py'=16] {'px','py'}, use_global_device_ids=true, to_apply=%region_41.0 | all-reduce | flops 3 | bytes 24 | tf_op jit(solution)/shard_map/psum | solution.py:89
  1253.5 74.1 %psum.141 = f32[]{:T(128)} all-reduce(f32[]{:T(128)} %multiply_reduce_fusion.4), channel_id=1, replica_groups=mesh['px'=16,'py'=16] {'px','py'}, use_global_device_ids=true, to_apply=%region_43.0 | all-reduce | flops 1 | bytes 8 | tf_op jit(solution)/shard_map/psum | solution.py:93
  1341.6 73.5 %all-reduce.20 = (f32[8]{0:T(128)S(1)}, f32[8]{0:T(128)S(1)}) all-reduce(f32[8]{0:T(128)S(1)} %get-tuple-element.148, f32[8]{0:T(128)S(1)} %get-tuple-element.147), channel_id=1, replica_groups=mesh['px'=16,'py'=16] {'px','py'}, use_global_device_ids=true, to_apply=%region_48.0 | all-reduce | flops 16 | bytes 128 | tf_op jit(solution)/shard_map/psum | solution.py:78
  1422.3 5.4 collective-permute-done.32
  (181 shorter events, 178.5 us)
Async XLA Ops:
  1.5 10.5 collective-permute-start
  4.2 6.8 collective-permute-start.1
  12.0 5.6 collective-permute-start.2
  100.6 6.5 collective-permute-start.5
  104.0 7.9 collective-permute-start.4
  270.2 7.1 collective-permute-start.9
  273.6 7.9 collective-permute-start.8
  281.5 5.1 collective-permute-start.10
  441.9 6.7 collective-permute-start.13
  445.3 7.9 collective-permute-start.12
  453.2 7.9 collective-permute-start.14
  455.1 6.0 collective-permute-start.15
  711.9 5.9 collective-permute-start.17
  715.2 7.9 collective-permute-start.16
  805.1 5.9 collective-permute-start.21
  808.5 7.9 collective-permute-start.20
  974.5 5.9 collective-permute-start.25
  977.9 7.9 collective-permute-start.24
  1146.1 6.7 collective-permute-start.29
  1149.5 7.9 collective-permute-start.28
  1158.1 7.9 collective-permute-start.30
  1160.0 6.0 collective-permute-start.31
  1416.4 5.9 collective-permute-start.33
  1419.8 7.9 collective-permute-start.32
  (15 other events, 271.5 us)
where the time goes:
time: 1440 us
  blocking collectives  1190 us (83%)
  starting transfers between devices  93.6 us (6%)
  waiting for transfers between devices  55.3 us (4%)
  other arithmetic  50.1 us (3%)
  between operations  27.2 us (2%)
  local copies, waits for them, and re-layouts  20.1 us (1%)
    psum x6, blocking collectives, local(): height = jnp.sqrt(lax.psum(jnp.sum(rest * rest), ('px', 'py')) + EPS)  445 us
    psum x6, blocking collectives, local(): summed = lax.psum(heights_local, ('px', 'py'))  444 us
    psum x4, blocking collectives, local(): lax.psum((dist_local, jnp.sum(force * force)), ('px', 'py'))  301 us
    ppermute x18, starting transfers between devices, extended(): lax.ppermute(tail, axis, [(i, (i + 1) % count) for i in range(ends)])  53.6 us
    ppermute x18, starting transfers between devices, extended(): lax.ppermute(head, axis, [((i + 1) % count, i) for i in range(ends)])  40 us
    ppermute x18, waiting for transfers between devices, extended(): lax.ppermute(head, axis, [((i + 1) % count, i) for i in range(ends)])  39.6 us
  transfers between devices with their start and end apart: 36, of which 16 were waited for; matrix products, arithmetic and copies ran while one was open for 1% of the time, Pallas kernels for 0%

commit v1 on v0

--- a/solution.py
+++ b/solution.py
@@ -86,7 +86,7 @@
             lap_basis.append(lap_vec)
             image = DIFFUSION * lap_vec + jac_diag * basis[k]
             heights_local = jnp.stack([jnp.sum(vec * image) for vec in basis])
-            summed = lax.psum(heights_local, ("px", "py"))
+            summed = lax.psum(lax.psum(heights_local, "py"), "px")
             rest = image
             for j in range(k + 1):
                 rest = rest - summed[j] * basis[j]

time: 1440 us -> 1330 us (0.924)
  blocking collectives: 1190 us -> 1080 us
    psum x6 -> x12, blocking collectives: 444 us -> 312 us  [local(): summed = lax.psum(lax.psum(heights_local, 'py'), 'px')]
    psum x6, blocking collectives: 445 us -> 475 us  [local(): height = jnp.sqrt(lax.psum(jnp.sum(rest * rest), ('px', 'py')) + EPS)]
  transfers between devices with their start and end apart: 36 -> 36, of which waited for: 16 -> 18; matrix products, arithmetic and copies ran while one was open for 1% -> 1% of each run, Pallas kernels for 0% -> 0%
where the time goes in v1:
time: 1330 us
  blocking collectives  1080 us (81%)
  starting transfers between devices  91.7 us (7%)
  waiting for transfers between devices  64.5 us (5%)
  other arithmetic  42.9 us (3%)
  between operations  27.6 us (2%)
  local copies, waits for them, and re-layouts  18.4 us (1%)
    psum x6, blocking collectives, local(): height = jnp.sqrt(lax.psum(jnp.sum(rest * rest), ('px', 'py')) + EPS)  475 us
    psum x12, blocking collectives, local(): summed = lax.psum(lax.psum(heights_local, 'py'), 'px')  312 us
    psum x4, blocking collectives, local(): lax.psum((dist_local, jnp.sum(force * force)), ('px', 'py'))  297 us
    ppermute x18, starting transfers between devices, extended(): lax.ppermute(tail, axis, [(i, (i + 1) % count) for i in range(ends)])  51.8 us
    ppermute x18, waiting for transfers between devices, extended(): lax.ppermute(head, axis, [((i + 1) % count, i) for i in range(ends)])  45.5 us
    ppermute x18, starting transfers between devices, extended(): lax.ppermute(head, axis, [((i + 1) % count, i) for i in range(ends)])  39.9 us
  transfers between devices with their start and end apart: 36, of which 18 were waited for; matrix products, arithmetic and copies ran while one was open for 1% of the time, Pallas kernels for 0%

profile of v1, /device:TPU:38, one launch (start us, length us, event | category | flops | bytes accessed | tf_op | source)
XLA Modules:
  0.0 1329.2 jit_solution(2875090072559103735)
XLA Ops:
  20.7 76.6 %psum.168 = f32[]{:T(128)} all-reduce(f32[]{:T(128)} %get-tuple-element.179), channel_id=1, replica_groups=mesh['px'=16,'py'=16] {'px','py'}, use_global_device_ids=true, to_apply=%region_1.0 | all-reduce | flops 1 | bytes 8 | tf_op jit(solution)/shard_map/psum | solution.py:78
  117.2 21.3 %psum.169 = f32[1]{0:T(128)} all-reduce(f32[1]{0:T(128)} %bitcast), channel_id=1, replica_groups=mesh['px'=16,'py'=16] {'py'}, use_global_device_ids=true, to_apply=%region_3.0 | all-reduce | flops 1 | bytes 8 | tf_op jit(solution)/shard_map/psum | solution.py:89
  139.2 31.0 %psum.170 = f32[1]{0:T(128)} all-reduce(f32[1]{0:T(128)} %psum.169), channel_id=1, replica_groups=mesh['px'=16,'py'=16] {'px'}, use_global_device_ids=true, to_apply=%region_4.0 | all-reduce | flops 1 | bytes 8 | tf_op jit(solution)/shard_map/psum | solution.py:89
  171.5 79.2 %psum.171 = f32[]{:T(128)} all-reduce(f32[]{:T(128)} %multiply_reduce_fusion.21), channel_id=1, replica_groups=mesh['px'=16,'py'=16] {'px','py'}, use_global_device_ids=true, to_apply=%region_6.0 | all-reduce | flops 1 | bytes 8 | tf_op jit(solution)/shard_map/psum | solution.py:93
  273.4 21.4 %psum.172 = f32[2]{0:T(128)S(1)} all-reduce(f32[2]{0:T(128)S(1)} %pad_maximum_fusion.92), channel_id=1, replica_groups=mesh['px'=16,'py'=16] {'py'}, use_global_device_ids=true, to_apply=%region_10.0 | all-reduce | flops 2 | bytes 16 | tf_op jit(solution)/shard_map/psum | solution.py:89
  294.8 30.4 %psum.173 = f32[2]{0:T(128)S(1)} all-reduce(f32[2]{0:T(128)S(1)} %psum.172), channel_id=1, replica_groups=mesh['px'=16,'py'=16] {'px'}, use_global_device_ids=true, to_apply=%region_11.0 | all-reduce | flops 2 | bytes 16 | tf_op jit(solution)/shard_map/psum | solution.py:89
  327.7 79.2 %psum.174 = f32[]{:T(128)} all-reduce(f32[]{:T(128)} %get-tuple-element.174), channel_id=1, replica_groups=mesh['px'=16,'py'=16] {'px','py'}, use_global_device_ids=true, to_apply=%region_13.0 | all-reduce | flops 1 | bytes 8 | tf_op jit(solution)/shard_map/psum | solution.py:93
  430.3 21.5 %psum.175 = f32[3]{0:T(128)S(1)} all-reduce(f32[3]{0:T(128)S(1)} %pad_maximum_fusion.93), channel_id=1, replica_groups=mesh['px'=16,'py'=16] {'py'}, use_global_device_ids=true, to_apply=%region_18.0 | all-reduce | flops 3 | bytes 24 | tf_op jit(solution)/shard_map/psum | solution.py:89
  452.0 30.4 %psum.176 = f32[3]{0:T(128)S(1)} all-reduce(f32[3]{0:T(128)S(1)} %psum.175), channel_id=1, replica_groups=mesh['px'=16,'py'=16] {'px'}, use_global_device_ids=true, to_apply=%region_19.0 | all-reduce | flops 3 | bytes 24 | tf_op jit(solution)/shard_map/psum | solution.py:89
  489.0 78.9 %psum.177 = f32[]{:T(128)} all-reduce(f32[]{:T(128)} %multiply_reduce_fusion.14), channel_id=1, replica_groups=mesh['px'=16,'py'=16] {'px','py'}, use_global_device_ids=true, to_apply=%region_21.0 | all-reduce | flops 1 | bytes 8 | tf_op jit(solution)/shard_map/psum | solution.py:93
  582.1 73.4 %all-reduce.21 = (f32[8]{0:T(128)S(1)}, f32[8]{0:T(128)S(1)}) all-reduce(f32[8]{0:T(128)S(1)} %get-tuple-element.150, f32[8]{0:T(128)S(1)} %get-tuple-element.149), channel_id=1, replica_groups=mesh['px'=16,'py'=16] {'px','py'}, use_global_device_ids=true, to_apply=%region_28.30 | all-reduce | flops 16 | bytes 128 | tf_op jit(solution)/shard_map/psum | solution.py:78
  676.4 73.7 %psum.180 = f32[]{:T(128)} all-reduce(f32[]{:T(128)} %get-tuple-element.171), channel_id=1, replica_groups=mesh['px'=16,'py'=16] {'px','py'}, use_global_device_ids=true, to_apply=%region_31.0 | all-reduce | flops 1 | bytes 8 | tf_op jit(solution)/shard_map/psum | solution.py:78
  756.6 5.4 collective-permute-done.20
  770.1 21.4 %psum.181 = f32[1]{0:T(128)} all-reduce(f32[1]{0:T(128)} %bitcast.32), channel_id=1, replica_groups=mesh['px'=16,'py'=16] {'py'}, use_global_device_ids=true, to_apply=%region_33.0 | all-reduce | flops 1 | bytes 8 | tf_op jit(solution)/shard_map/psum | solution.py:89
  791.5 31.2 %psum.182 = f32[1]{0:T(128)} all-reduce(f32[1]{0:T(128)} %psum.181), channel_id=1, replica_groups=mesh['px'=16,'py'=16] {'px'}, use_global_device_ids=true, to_apply=%region_34.0 | all-reduce | flops 1 | bytes 8 | tf_op jit(solution)/shard_map/psum | solution.py:89
  824.0 79.6 %psum.183 = f32[]{:T(128)} all-reduce(f32[]{:T(128)} %multiply_reduce_fusion.11), channel_id=1, replica_groups=mesh['px'=16,'py'=16] {'px','py'}, use_global_device_ids=true, to_apply=%region_36.0 | all-reduce | flops 1 | bytes 8 | tf_op jit(solution)/shard_map/psum | solution.py:93
  910.9 5.4 collective-permute-done.24
  926.3 21.4 %psum.184 = f32[2]{0:T(128)S(1)} all-reduce(f32[2]{0:T(128)S(1)} %pad_maximum_fusion.94), channel_id=1, replica_groups=mesh['px'=16,'py'=16] {'py'}, use_global_device_ids=true, to_apply=%region_39.0 | all-reduce | flops 2 | bytes 16 | tf_op jit(solution)/shard_map/psum | solution.py:89
  947.8 30.4 %psum.185 = f32[2]{0:T(128)S(1)} all-reduce(f32[2]{0:T(128)S(1)} %psum.184), channel_id=1, replica_groups=mesh['px'=16,'py'=16] {'px'}, use_global_device_ids=true, to_apply=%region_40.0 | all-reduce | flops 2 | bytes 16 | tf_op jit(solution)/shard_map/psum | solution.py:89
  980.7 78.6 %psum.186 = f32[]{:T(128)} all-reduce(f32[]{:T(128)} %get-tuple-element.166), channel_id=1, replica_groups=mesh['px'=16,'py'=16] {'px','py'}, use_global_device_ids=true, to_apply=%region_42.0 | all-reduce | flops 1 | bytes 8 | tf_op jit(solution)/shard_map/psum | solution.py:93
  1082.5 21.5 %psum.187 = f32[3]{0:T(128)S(1)} all-reduce(f32[3]{0:T(128)S(1)} %pad_maximum_fusion.95), channel_id=1, replica_groups=mesh['px'=16,'py'=16] {'py'}, use_global_device_ids=true, to_apply=%region_46.0 | all-reduce | flops 3 | bytes 24 | tf_op jit(solution)/shard_map/psum | solution.py:89
  1104.2 30.4 %psum.188 = f32[3]{0:T(128)S(1)} all-reduce(f32[3]{0:T(128)S(1)} %psum.187), channel_id=1, replica_groups=mesh['px'=16,'py'=16] {'px'}, use_global_device_ids=true, to_apply=%region_47.0 | all-reduce | flops 3 | bytes 24 | tf_op jit(solution)/shard_map/psum | solution.py:89
  1141.2 79.4 %psum.189 = f32[]{:T(128)} all-reduce(f32[]{:T(128)} %multiply_reduce_fusion.4), channel_id=1, replica_groups=mesh['px'=16,'py'=16] {'px','py'}, use_global_device_ids=true, to_apply=%region_49.0 | all-reduce | flops 1 | bytes 8 | tf_op jit(solution)/shard_map/psum | solution.py:93
  1234.8 73.4 %all-reduce.20 = (f32[8]{0:T(128)S(1)}, f32[8]{0:T(128)S(1)}) all-reduce(f32[8]{0:T(128)S(1)} %get-tuple-element.148, f32[8]{0:T(128)S(1)} %get-tuple-element.147), channel_id=1, replica_groups=mesh['px'=16,'py'=16] {'px','py'}, use_global_device_ids=true, to_apply=%region_54.0 | all-reduce | flops 16 | bytes 128 | tf_op jit(solution)/shard_map/psum | solution.py:78
  (189 shorter events, 206.7 us)
Async XLA Ops:
  1.5 5.8 collective-permute-start.1
  4.9 7.9 collective-permute-start
  12.8 5.5 collective-permute-start.2
  14.8 5.1 collective-permute-start.3
  98.1 6.5 collective-permute-start.5
  101.4 7.9 collective-permute-start.4
  252.1 7.2 collective-permute-start.9
  255.5 7.9 collective-permute-start.8
  407.7 6.0 collective-permute-start.13
  411.0 7.9 collective-permute-start.12
  419.0 6.3 collective-permute-start.14
  656.8 5.9 collective-permute-start.17
  660.1 7.9 collective-permute-start.16
  670.1 5.5 collective-permute-start.19
  750.8 5.9 collective-permute-start.21
  754.1 7.9 collective-permute-start.20
  905.0 5.9 collective-permute-start.25
  908.4 7.9 collective-permute-start.24
  1060.0 6.0 collective-permute-start.29
  1063.4 7.9 collective-permute-start.28
  1071.3 6.3 collective-permute-start.30
  1309.6 5.9 collective-permute-start.33
  1312.9 7.9 collective-permute-start.32
  1322.8 5.5 collective-permute-start.35
  (16 other events, 355.3 us)
